TPU v7x, 32 devices: a whole 2x2x4 slice. The times are simulated.
32 devices in a mesh: rep: 2 (over x), shard: 16 (over z, y, core).
Axes of the slice: x: 2, y: 2, z: 4, core: 2. Of those that a mesh axis runs over, the one named last changes fastest.
Arguments:
- tokens: bfloat16 [32, 192, 2048], P(('rep', 'shard')), may hold values from -7 to 7
- segment_ids: int32 [32, 192], P(('rep', 'shard')), may hold values from 0 to 3, never falling along the last dimension, each value on 1 to 96 neighbouring positions
- norm_gain: bfloat16 [2048], P('shard'), may hold values from 0.25 to 1.75
- input_weight: bfloat16 [2048, 2048], P('shard'), may hold values from -0.125 to 0.125
- forget_weight: bfloat16 [2048, 2048], P('shard'), may hold values from -0.5 to 0.5
- gate_weight: bfloat16 [2048, 2048], P('shard'), may hold values from -0.125 to 0.125
- mixer_gain: bfloat16 [2048], P('shard'), may hold values from 0.25 to 1.75
- out_weight: bfloat16 [2048, 2048], P('shard'), may hold values from -0.1875 to 0.1875
- ffn_gain: bfloat16 [2048], P('shard'), may hold values from 0.25 to 1.75
- ffn_gate_weight: bfloat16 [2048, 5632], P('shard'), may hold values from -0.125 to 0.125
- ffn_up_weight: bfloat16 [2048, 5632], P('shard'), may hold values from -0.125 to 0.125
- ffn_down_weight: bfloat16 [5632, 2048], P('shard'), may hold values from -0.15625 to 0.15625
- cotangent: bfloat16 [32, 192, 2048], P(('rep', 'shard')), may hold values from -6 to 6
Outputs:
- block_output: bfloat16 [32, 192, 2048], P(('rep', 'shard'))
- input_grad: bfloat16 [32, 192, 2048], P(('rep', 'shard'))
- norm_gain_grad: float32 [2048], P('shard')
- input_weight_grad: float32 [2048, 2048], P('shard')
- forget_weight_grad: float32 [2048, 2048], P('shard')
- gate_weight_grad: float32 [2048, 2048], P('shard')
- mixer_gain_grad: float32 [2048], P('shard')
- out_weight_grad: float32 [2048, 2048], P('shard')
- ffn_gain_grad: float32 [2048], P('shard')
- ffn_gate_grad: float32 [2048, 5632], P('shard')
- ffn_up_grad: float32 [2048, 5632], P('shard')
- ffn_down_grad: float32 [5632, 2048], P('shard')
Inputs may be any that keep to these rules, and one draw needn't show every extreme that they name: `segment_ids`: document numbers never fall along a sequence; each document has 1 to 96 tokens, and one has exactly 96.
All inputs are finite; a program needn't handle non-finite values.
Results may differ from a plain program's by a relative error of at most 0.019.
Values may be sent and summed in bfloat16 or wider, within the bound.
No kernel may reach another device: no remote copies, remote signals or barrier semaphores. Data moves between devices by JAX's collectives and lax.ppermute only.
A program may use at most 640 MiB of HBM per device.

v0:
```python
import jax
import jax.numpy as jnp
from jax import lax
from jax.sharding import PartitionSpec as P

EPSILON = 1e-06


def normalize(values):
    scale = lax.rsqrt(jnp.mean(values * values, axis=-1, keepdims=True) + EPSILON)
    return (values * scale, scale)


def norm_back(grad_scaled, scaled, scale):
    inner = jnp.mean(grad_scaled * scaled, axis=-1, keepdims=True)
    return scale * (grad_scaled - scaled * inner)


def swish_pair(values):
    sigma = jax.nn.sigmoid(values)
    return (values * sigma, sigma * (1.0 + values * (1.0 - sigma)))


def combine_steps(earlier, later):
    return (earlier[0] * later[0], later[0] * earlier[1] + later[1])


def linear_scan(decay, update):
    return lax.associative_scan(combine_steps, (decay, update), axis=0)[1]


def contract_rows(left, piece):
    return lax.dot_general(
        left, piece, (((1,), (1,)), ((), ())), preferred_element_type=jnp.float32
    )


def gain_folder(scaled, carry, pieces):
    sums, fulls, gain_full = carry
    gain_piece = pieces[-1]
    matrices = pieces[:-1]
    columns = scaled * gain_piece.astype(jnp.float32)
    lowered = columns.astype(jnp.bfloat16)
    sums = tuple(
        (jnp.dot(lowered, piece, preferred_element_type=jnp.float32) for piece in matrices)
    )
    gain_full = gain_piece
    return (sums, fulls, gain_full)


def plain_folder(lowered_rows, carry, piece):
    total, full = carry
    total = jnp.dot(lowered_rows, piece, preferred_element_type=jnp.float32)
    return (total, full)


def start_carry(length, width, columns, number):
    sums = tuple((jnp.zeros((length, columns), jnp.float32) for index in range(number)))
    fulls = ()
    return (sums, fulls, jnp.zeros((width,), jnp.bfloat16))


def single_columns(left, piece):
    return contract_rows(left, piece)


def multi_columns(lefts, pieces):
    total = contract_rows(lefts[0], pieces[0])
    for left, piece in zip(lefts[1:], pieces[1:]):
        total = total + contract_rows(left, piece)
    return total


def row_grad(left, right):
    return lax.dot_general(
        left, right, (((0,), (0,)), ((), ())), preferred_element_type=jnp.float32
    )


def row_block(pairs, gains):
    pieces = [row_grad(left, right) for left, right in pairs]
    pieces = pieces + [vector[:, None] for vector in gains]
    return jnp.concatenate(pieces, axis=1)


def shards(
    tokens,
    segment_ids,
    norm_gain,
    input_weight,
    forget_weight,
    gate_weight,
    mixer_gain,
    out_weight,
    ffn_gain,
    ffn_gate_weight,
    ffn_up_weight,
    ffn_down_weight,
    cotangent,
):
    inputs = tokens[0].astype(jnp.float32)
    length, width = inputs.shape
    hidden_width = ffn_up_weight.shape[1]
    segments = segment_ids[0]
    same = jnp.concatenate(
        [jnp.zeros((1,), jnp.float32), (segments[1:] == segments[:-1]).astype(jnp.float32)]
    )
    scaled_in, scale_in = normalize(inputs)
    mixer_sums, mixer_full, gain_one = gain_folder(
        scaled_in,
        start_carry(length, width, width, 3),
        (
            lax.all_gather(input_weight, "shard", axis=0, tiled=True),
            lax.all_gather(forget_weight, "shard", axis=0, tiled=True),
            lax.all_gather(gate_weight, "shard", axis=0, tiled=True),
            lax.all_gather(norm_gain, "shard", axis=0, tiled=True),
        ),
    )
    input_pre, forget_pre, gate_pre = mixer_sums
    forget = jax.nn.sigmoid(forget_pre)
    input_act, input_slope = swish_pair(input_pre)
    update = input_act * (1.0 - forget)
    decay = forget * same[:, None]
    state = linear_scan(decay, update)
    state_scaled, state_scale = normalize(state)
    gate_act, gate_slope = swish_pair(gate_pre)
    mixed_pre = state_scaled * gate_act
    out_sums, out_full, gain_two = gain_folder(
        mixed_pre,
        start_carry(length, width, width, 1),
        (
            lax.all_gather(out_weight, "shard", axis=0, tiled=True),
            lax.all_gather(mixer_gain, "shard", axis=0, tiled=True),
        ),
    )
    resid = inputs + out_sums[0]
    scaled_mid, scale_mid = normalize(resid)
    ffn_sums, ffn_full, gain_three = gain_folder(
        scaled_mid,
        start_carry(length, width, hidden_width, 2),
        (
            lax.all_gather(ffn_gate_weight, "shard", axis=0, tiled=True),
            lax.all_gather(ffn_up_weight, "shard", axis=0, tiled=True),
            lax.all_gather(ffn_gain, "shard", axis=0, tiled=True),
        ),
    )
    ffn_gate, ffn_up = ffn_sums
    ffn_act, ffn_slope = swish_pair(ffn_gate)
    hidden = (ffn_act * ffn_up).astype(jnp.bfloat16)
    down_start = (jnp.zeros((length, width), jnp.float32), jnp.zeros((1, 1), jnp.bfloat16))
    ffn_out, down_full = plain_folder(
        hidden, down_start, lax.all_gather(ffn_down_weight, "shard", axis=0, tiled=True)
    )
    block_output = (resid + ffn_out).astype(jnp.bfloat16)
    grad_out = cotangent[0]
    grad_hidden = single_columns(
        grad_out, lax.all_gather(ffn_down_weight, "shard", axis=0, tiled=True)
    )
    grad_fgate = (grad_hidden * ffn_up * ffn_slope).astype(jnp.bfloat16)
    grad_fup = (grad_hidden * ffn_act).astype(jnp.bfloat16)
    grad_ffn_in = multi_columns(
        (grad_fgate, grad_fup),
        lax.all_gather((ffn_gate_weight, ffn_up_weight), "shard", axis=0, tiled=True),
    )
    gain_three_f = gain_three.astype(jnp.float32)
    mid_low = (scaled_mid * gain_three_f).astype(jnp.bfloat16)
    gain_three_grad = jnp.sum(grad_ffn_in * scaled_mid, axis=0)
    grad_resid = grad_out.astype(jnp.float32) + norm_back(
        grad_ffn_in * gain_three_f, scaled_mid, scale_mid
    )
    grad_branch = grad_resid.astype(jnp.bfloat16)
    grad_mixed = single_columns(
        grad_branch, lax.all_gather(out_weight, "shard", axis=0, tiled=True)
    )
    gain_two_f = gain_two.astype(jnp.float32)
    mixed_low = (mixed_pre * gain_two_f).astype(jnp.bfloat16)
    gain_two_grad = jnp.sum(grad_mixed * mixed_pre, axis=0)
    weighted = grad_mixed * gain_two_f
    grad_gate_pre = (weighted * state_scaled * gate_slope).astype(jnp.bfloat16)
    grad_state = norm_back(weighted * gate_act, state_scaled, state_scale)
    next_decay = jnp.concatenate([decay[1:], jnp.zeros((1, width), jnp.float32)])
    carried = jnp.flip(linear_scan(jnp.flip(next_decay, 0), jnp.flip(grad_state, 0)), 0)
    previous = jnp.concatenate([jnp.zeros((1, width), jnp.float32), state[:-1]])
    grad_forget = carried * previous * same[:, None] - carried * input_act
    grad_input_pre = (carried * (1.0 - forget) * input_slope).astype(jnp.bfloat16)
    grad_forget_pre = (grad_forget * forget * (1.0 - forget)).astype(jnp.bfloat16)
    triple = (grad_input_pre, grad_forget_pre, grad_gate_pre)
    grad_normed = multi_columns(
        triple,
        lax.all_gather((input_weight, forget_weight, gate_weight), "shard", axis=0, tiled=True),
    )
    gain_one_f = gain_one.astype(jnp.float32)
    in_low = (scaled_in * gain_one_f).astype(jnp.bfloat16)
    gain_one_grad = jnp.sum(grad_normed * scaled_in, axis=0)
    input_grad = (grad_resid + norm_back(grad_normed * gain_one_f, scaled_in, scale_in)).astype(
        jnp.bfloat16
    )
    triple_joined = jnp.concatenate(triple, axis=1)
    pair_joined = jnp.concatenate([grad_fgate, grad_fup], axis=1)
    pairs = ((in_low, triple_joined), (mixed_low, grad_branch), (mid_low, pair_joined))
    gains = (gain_one_grad, gain_two_grad, gain_three_grad)
    rows_term = lax.psum_scatter(
        row_block(pairs, gains).astype(jnp.bfloat16), "shard", scatter_dimension=0, tiled=True
    )
    down_term = lax.psum_scatter(
        row_grad(hidden, grad_out).astype(jnp.bfloat16), "shard", scatter_dimension=0, tiled=True
    )
    rows_total, down_total = (
        lax.psum(rows_term, "rep").astype(jnp.float32),
        lax.psum(down_term, "rep").astype(jnp.float32),
    )
    tail = 4 * width + 2 * hidden_width
    return (
        block_output[None],
        input_grad[None],
        rows_total[:, tail],
        rows_total[:, :width],
        rows_total[:, width : 2 * width],
        rows_total[:, 2 * width : 3 * width],
        rows_total[:, tail + 1],
        rows_total[:, 3 * width : 4 * width],
        rows_total[:, tail + 2],
        rows_total[:, 4 * width : 4 * width + hidden_width],
        rows_total[:, 4 * width + hidden_width : tail],
        down_total,
    )


def solution(mesh):
    placed = (
        P(("rep", "shard"), None, None),
        P(("rep", "shard"), None),
        P("shard"),
        P("shard", None),
        P("shard", None),
        P("shard", None),
        P("shard"),
        P("shard", None),
        P("shard"),
        P("shard", None),
        P("shard", None),
        P("shard", None),
        P(("rep", "shard"), None, None),
    )
    return jax.shard_map(
        shards,
        mesh=mesh,
        in_specs=placed,
        out_specs=(
            P(("rep", "shard"), None, None),
            P(("rep", "shard"), None, None),
            P("shard"),
            P("shard", None),
            P("shard", None),
            P("shard", None),
            P("shard"),
            P("shard", None),
            P("shard"),
            P("shard", None),
            P("shard", None),
            P("shard", None),
        ),
        check_vma=False,
    )
```

profile of v0, /device:TPU:0, one launch (start us, length us, event | category | flops | bytes accessed | tf_op | source)
XLA Modules:
  0.0 2012.6 jit_solution(17651145178794768228)
XLA Ops:
  12.0 23.2 %all-gather = bf16[16,1,128]{2,1,0:T(2,128)(2,1)S(1)} all-gather(bf16[1,1,128]{2,1,0:T(2,128)(2,1)S(1)} %bitcast.75), channel_id=1, replica_groups=mesh['rep'=2,'shard'=16] {'shard'}, dimensions={0}, use_global_device_ids=true | all-gather | bytes 4352 | tf_op jit(solution)/shard_map/all_gather | solution.py:116
  35.2 17.5 all-gather.1
  52.7 18.9 all-gather.2
  72.6 15.3 all-gather.11.cloned.1.call-done
  87.9 6.4 fusion.57
  94.3 69.0 %all-gather.13.cloned.1.call-done = bf16[2048,2048]{1,0:T(8,128)(2,1)} async-done(((bf16[128,2048]{1,0:T(8,128)(2,1)}), bf16[2048,2048]{1,0:T(8,128)(2,1)}) %all-gather.13.cloned.1.call-update) | async-done | bytes 8388624 | tf_op jit(solution)/shard_map/all_gather | solution.py:114
  163.3 7.8 broadcast_multiply_fusion
  171.4 2.2 slice.394
  173.6 2.2 slice.393
  177.4 4.4 slice.444
  181.9 2.1 slice.396
  184.0 2.1 slice.395
  186.2 1.6 fusion.62
  196.7 2.4 pad.101
  200.5 38.1 %all-gather.15.cloned.1.call-done = bf16[2048,2048]{1,0:T(8,128)(2,1)} async-done(((bf16[128,2048]{1,0:T(8,128)(2,1)}), bf16[2048,2048]{1,0:T(8,128)(2,1)}) %all-gather.15.cloned.1.call-update) | async-done | bytes 8388624 | tf_op jit(solution)/shard_map/all_gather | solution.py:115
  238.6 7.6 multiply_multiply_fusion.1
  246.2 67.6 %all-gather.17.cloned.1.call-done = bf16[2048,2048]{1,0:T(8,128)(2,1)} async-done(((bf16[128,2048]{1,0:T(8,128)(2,1)}), bf16[2048,2048]{1,0:T(8,128)(2,1)}) %all-gather.17.cloned.1.call-update) | async-done | bytes 8388624 | tf_op jit(solution)/shard_map/all_gather | solution.py:132
  313.8 5.9 multiply_reduce_fusion.4
  322.0 110.3 %all-gather.21.cloned.1.call-done = bf16[2048,5632]{1,0:T(8,128)(2,1)} async-done(((bf16[128,5632]{1,0:T(8,128)(2,1)}), bf16[2048,5632]{1,0:T(8,128)(2,1)}) %all-gather.21.cloned.1.call-update) | async-done | bytes 23068688 | tf_op jit(solution)/shard_map/all_gather | solution.py:143
  432.3 14.5 fusion.74
  446.8 105.7 %all-gather.19.cloned.1.call-done = bf16[2048,5632]{1,0:T(8,128)(2,1)} async-done(((bf16[128,5632]{1,0:T(8,128)(2,1)}), bf16[2048,5632]{1,0:T(8,128)(2,1)}) %all-gather.19.cloned.1.call-update) | async-done | bytes 23068688 | tf_op jit(solution)/shard_map/all_gather | solution.py:142
  552.4 14.7 fusion.73
  567.1 105.7 %all-gather.23.cloned.1.call-done = bf16[5632,2048]{1,0:T(8,128)(2,1)} async-done(((bf16[352,2048]{1,0:T(8,128)(2,1)}), bf16[5632,2048]{1,0:T(8,128)(2,1)}) %all-gather.23.cloned.1.call-update) | async-done | bytes 23068688 | tf_op jit(solution)/shard_map/all_gather | solution.py:152
  672.8 16.0 multiply_convert_fusion
  690.1 10.9 convolution_convert_fusion.1
  703.9 4.4 slice.456
  708.3 4.5 slice.449
  712.8 4.5 slice.447
  717.3 8.6 slice.457
  725.9 8.7 slice.448
  734.6 8.6 slice.450
  745.4 12.1 fusion.75
  757.6 14.4 multiply_reduce_fusion
  772.0 2.2 multiply_add_fusion
  775.2 8.6 multiply_reduce_fusion.1
  785.0 2.1 slice.503
  787.1 2.1 slice.453
  789.3 2.1 slice.451
  791.4 8.6 slice.452
  800.1 5.1 slice.454
  805.1 2.1 fusion.61
  821.1 1.8 broadcast_in_dim.19
  822.9 1.8 broadcast_in_dim.20
  824.8 5.5 slice.504
  836.3 2.3 pad.114
  838.6 5.2 pad.115
  843.8 2.8 add.313
  846.6 16.0 rev.6
  862.6 4.1 multiply_convert_fusion.4
  866.8 6.8 fusion.76
  873.7 2.9 convolution_add_fusion.1
  876.7 4.3 fusion.24
  882.1 5.8 convolution_convert_fusion.3
  887.9 12.3 copy.30
  900.2 13.6 convolution_convert_fusion.2
  913.7 20.9 %convolution_convert_fusion = bf16[2048,11264]{1,0:T(8,128)(2,1)} fusion(bf16[192,2048]{1,0:T(8,128)(2,1)} %multiply_convert_fusion.6, bf16[192,5632]{1,0:T(8,128)(2,1)} %get-tuple-element.29, bf16[192,5632]{1,0:T(8,128)(2,1)} %get-tuple-element.30), kind=kOutput, calls=%fused_computation | convolution fusion | flops 8890089472 | bytes 51249152 | tf_op jit(solution)/shard_map/dot_general | solution.py:75
  934.6 158.1 %concatenate.84 = bf16[2048,19459]{1,0:T(8,128)(2,1)} concatenate(bf16[2048,6144]{1,0:T(8,128)(2,1)} %convolution_convert_fusion.2, bf16[2048,2048]{1,0:T(8,128)(2,1)} %copy.30, bf16[2048,11264]{1,0:T(8,128)(2,1)} %convolution_convert_fusion, bf16[2048,1]{1,0:T(8,128)(2,1)} %broadcast_in_dim.18, bf16[2048,1]{1,0:T(8,128)(2,1)S(1)} %copy-done.24, bf16[2048,1]{1,0:T(8,128)(2,1)S(1)} %copy-done.25), dimensions={1} | concatenate | bytes 159408128 | tf_op jit(solution)/shard_map/concatenate | solution.py:83
  1092.8 743.0 %reduce-scatter.3.cloned.1.call-done = bf16[128,19459]{1,0:T(8,128)(2,1)} async-done(((bf16[2048,19459]{1,0:T(8,128)(2,1)}), bf16[128,19459]{1,0:T(8,128)(2,1)}) %reduce-scatter.3.cloned.1.call-update) | async-done | bytes 4981520 | tf_op jit(solution)/shard_map/reduce_scatter | solution.py:202
  1835.9 2.9 fusion.28
  1838.7 12.3 fusion.8
  1851.0 143.4 %all-reduce.33.cloned.1.call-done = (bf16[128,19459]{1,0:T(8,128)(2,1)}, bf16[352,2048]{1,0:T(8,128)(2,1)}) async-done(((bf16[128,19459]{1,0:T(8,128)(2,1)}, bf16[352,2048]{1,0:T(8,128)(2,1)}), (bf16[128,19459]{1,0:T(8,128)(2,1)}, bf16[352,2048]{1,0:T(8,128)(2,1)})) %all-reduce.33.cloned.1.call-update) | async-done | bytes 6423312 | tf_op jit(solution)/shard_map/psum | solution.py:209
  1994.4 3.8 fusion.60
  1998.3 3.2 fusion.59
  2002.9 1.9 convert_element_type.95
  (294 shorter events, 51.2 us)
Async XLA Ops:
  7.2 80.7 %all-gather.11.cloned.1.call-start = ((), (), s32[]{:S(2)}) async-start(), calls=%async_computation.2 | async-start | bytes 8912896 | tf_op jit(solution)/shard_map/all_gather | solution.py:113
  7.9 155.3 %all-gather.13.cloned.1.call-start = ((), (), s32[]{:S(2)}) async-start(), calls=%async_computation.3 | async-start | bytes 8912896 | tf_op jit(solution)/shard_map/all_gather | solution.py:114
  8.7 229.9 %all-gather.15.cloned.1.call-start = ((), (), s32[]{:S(2)}) async-start(), calls=%async_computation.4 | async-start | bytes 8912896 | tf_op jit(solution)/shard_map/all_gather | solution.py:115
  9.4 304.4 %all-gather.17.cloned.1.call-start = ((), (), s32[]{:S(2)}) async-start(), calls=%async_computation.5 | async-start | bytes 8912896 | tf_op jit(solution)/shard_map/all_gather | solution.py:132
  10.0 422.3 %all-gather.21.cloned.1.call-start = ((), (), s32[]{:S(2)}) async-start(), calls=%async_computation.7 | async-start | bytes 24510464 | tf_op jit(solution)/shard_map/all_gather | solution.py:143
  10.6 1.4 copy-start.45
  10.6 24.7 %copy-start.46 = (bf16[128]{0:T(256)(128)(2,1)S(1)}, bf16[128]{0:T(256)(128)(2,1)}, u32[]{:S(2)}) copy-start(bf16[128]{0:T(256)(128)(2,1)} %param.19) | copy-start | bytes 772
  10.6 42.1 %copy-start.47 = (bf16[128]{0:T(256)(128)(2,1)S(1)}, bf16[128]{0:T(256)(128)(2,1)}, u32[]{:S(2)}) copy-start(bf16[128]{0:T(256)(128)(2,1)} %param.21) | copy-start | bytes 772
  10.6 61.6 %copy-start.44 = (s32[1,192]{1,0:T(1,128)S(1)}, s32[1,192]{1,0:T(1,128)}, u32[]{:S(2)}) copy-start(s32[1,192]{1,0:T(1,128)} %param.14) | copy-start | bytes 2308
  10.6 61.8 %copy-start.1 = (bf16[1,192,2048]{2,1,0:T(8,128)(2,1)S(1)}, bf16[1,192,2048]{2,1,0:T(8,128)(2,1)}, u32[]{:S(2)}) copy-start(bf16[1,192,2048]{2,1,0:T(8,128)(2,1)} %param.13) | copy-start | bytes 2359300
  10.6 541.8 %all-gather.19.cloned.1.call-start = ((), (), s32[]{:S(2)}) async-start(), calls=%async_computation.6 | async-start | bytes 24510464 | tf_op jit(solution)/shard_map/all_gather | solution.py:142
  11.2 661.6 %all-gather.23.cloned.1.call-start = ((), (), s32[]{:S(2)}) async-start(), calls=%async_computation.8 | async-start | bytes 24510464 | tf_op jit(solution)/shard_map/all_gather | solution.py:152
  11.9 1080.8 %reduce-scatter.5.cloned.1.call-start = ((), (), s32[]{:S(2)}) async-start(), calls=%async_computation.10 | async-start | bytes 24510464 | tf_op jit(solution)/shard_map/reduce_scatter | solution.py:205
  72.4 90.9 %copy-start.42 = (f32[192]{0:T(256)}, f32[192]{0:T(256)S(1)}, u32[]{:S(2)}) copy-start(f32[192]{0:T(256)S(1)} %add_convert_fusion) | copy-start | bytes 2308
  72.6 90.6 %copy-start.32 = (f32[192]{0:T(256)}, f32[192]{0:T(256)S(1)}, u32[]{:S(2)}) copy-start(f32[192]{0:T(256)S(1)} %add_rsqrt_fusion.2) | copy-start | bytes 2308
  171.0 2.6 copy-start.3
  175.9 6.0 copy-start.10
  181.9 4.3 copy-start.13
  193.2 0.7 copy-start.38
  194.1 1.1 copy-start.17
  194.1 1.6 copy-start.18
  195.7 0.7 copy-start.36
  199.1 39.5 %copy-start.33 = (f32[192]{0:T(256)S(1)}, f32[192]{0:T(256)}, u32[]{:S(2)}) copy-start(f32[192]{0:T(256)} %copy-done.32) | copy-start | bytes 2308
  313.8 7.1 copy-start.31
  319.7 1.2 copy-start.5
  672.8 17.3 copy-start.20
  688.8 1.3 copy-start.8
  701.1 1134.7 %reduce-scatter.3.cloned.1.call-start = ((), (), s32[]{:S(2)}) async-start(), calls=%async_computation.9 | async-start | bytes 85229568 | tf_op jit(solution)/shard_map/reduce_scatter | solution.py:202
  743.2 2.2 copy-start.23
  745.4 12.2 copy-start.6
  772.0 2.2 copy-start.4
  772.0 2.7 copy-start.21
  772.0 3.2 copy-start.27
  791.4 8.7 copy-start.15
  810.3 3.6 copy-start.26
  819.0 5.8 copy-start.14
  822.9 7.7 copy-start.41
  830.3 0.7 copy-start.40
  830.8 0.7 copy-start.39
  831.5 1.0 copy-start.28
  831.5 1.1 copy-start.29
  831.6 1.0 copy-start.37
  832.9 1.4 copy-start.16
  832.9 1.7 copy-start.19
  834.6 0.7 copy-start.35
  846.6 16.0 copy-start.43
  862.6 11.0 slice-start
  866.8 6.9 copy-start.12
  866.8 6.9 slice-start.1
  866.8 9.8 slice-start.2
  873.7 2.9 copy-start.2
  873.7 2.9 slice-start.3
  873.7 2.9 copy-start.11
  873.7 2.9 copy-start.34
  876.6 5.4 copy-start.22
  913.7 20.9 %copy-start.24 = (bf16[2048,1]{1,0:T(8,128)(2,1)S(1)}, bf16[2048,1]{1,0:T(8,128)(2,1)}, u32[]{:S(2)}) copy-start(bf16[2048,1]{1,0:T(8,128)(2,1)} %broadcast_in_dim.19) | copy-start | bytes 12292
  913.7 20.9 %copy-start.25 = (bf16[2048,1]{1,0:T(8,128)(2,1)S(1)}, bf16[2048,1]{1,0:T(8,128)(2,1)}, u32[]{:S(2)}) copy-start(bf16[2048,1]{1,0:T(8,128)(2,1)} %broadcast_in_dim.20) | copy-start | bytes 12292
  1092.7 901.7 %all-reduce.33.cloned.1.call-start = ((), (), s32[]{:S(2)}) async-start(), calls=%async_computation.11 | async-start | bytes 12910592 | tf_op jit(solution)/shard_map/psum | solution.py:209
  1835.8 2.9 copy-start.7
  1835.9 2.9 copy-start.9
  1994.4 3.9 copy-start
  2001.5 1.4 copy-start.30
Sparse Core Ops, SparseCore 0:
  10.2 77.6 all-gather.10
  90.1 73.1 all-gather.12
  165.4 73.1 all-gather.14
  240.6 73.1 all-gather.16
  315.3 116.9 all-gather.20
  433.7 118.6 all-gather.18
  554.0 118.6 all-gather.22
  701.2 226.8 reduce-scatter.4
  1092.8 742.9 reduce-scatter.2
  1838.2 156.2 all-reduce.32
where the time goes:
time: 2030 us; the launch traced here: 2010 us
  waiting for transfers between devices  1400 us (69%)
  local copies, waits for them, and re-layouts  319 us (16%)
  matrix products  185 us (9%)
  blocking collectives  59.6 us (3%)
  other arithmetic  30.4 us (1%)
    reduce_scatter x1, waiting for transfers between devices, shards(): lax.psum_scatter(row_block(pairs, gains).astype(jnp.bfloat16), 'shard', s...  743 us
    concatenate x1, local copies, waits for them, and re-layouts, row_block(): return jnp.concatenate(pieces, axis=1)  158 us
    psum x1, waiting for transfers between devices, shards(): lax.psum(rows_term, 'rep').astype(jnp.float32)  143 us
    all_gather x1, waiting for transfers between devices, shards(): lax.all_gather(ffn_up_weight, 'shard', axis=0, tiled=True)  110 us
    all_gather x1, waiting for transfers between devices, shards(): lax.all_gather(ffn_gate_weight, 'shard', axis=0, tiled=True)  106 us
    all_gather x1, waiting for transfers between devices, shards(): lax.all_gather(ffn_down_weight, 'shard', axis=0, tiled=True)  106 us
    slice x90, local copies, waits for them, and re-layouts, linear_scan(): return lax.associative_scan(combine_steps, (decay, update), axis=0)[1]  96.4 us
    all_gather x1, waiting for transfers between devices, shards(): lax.all_gather(forget_weight, 'shard', axis=0, tiled=True)  69 us
  transfers between devices with their start and end apart: 10, of which 9 were waited for; matrix products, arithmetic and copies ran while one was open for 24% of the time, Pallas kernels for 0%

commit v1 on v0

--- a/solution.py
+++ b/solution.py
@@ -206,7 +206,7 @@
         row_grad(hidden, grad_out).astype(jnp.bfloat16), "shard", scatter_dimension=0, tiled=True
     )
     rows_total, down_total = (
-        lax.psum(rows_term, "rep").astype(jnp.float32),
+        jnp.sum(lax.all_gather(rows_term, "rep"), axis=0).astype(jnp.float32),
         lax.psum(down_term, "rep").astype(jnp.float32),
     )
     tail = 4 * width + 2 * hidden_width

time: 2030 us -> 2120 us (1.044)
  local copies, waits for them, and re-layouts: 319 us -> 413 us
  waiting for transfers between devices: 1400 us -> 1360 us
  other arithmetic: 30.4 us -> 63.6 us
    all_gather x0 -> x1, waiting for transfers between devices: none -> 123 us  [shards(): lax.all_gather(rows_term, 'rep')]
    psum x1, waiting for transfers between devices: 143 us -> 35.3 us  [shards(): lax.psum(down_term, 'rep').astype(jnp.float32)]
    slice x90, local copies, waits for them, and re-layouts: 96.4 us -> 194 us  [linear_scan(): return lax.associative_scan(combine_steps, (decay, update), axis=0)[1]]
    all_gather x1, waiting for transfers between devices: 38.1 us -> 0.01 us  [shards(): lax.all_gather(gate_weight, 'shard', axis=0, tiled=True)]
  transfers between devices with their start and end apart: 10 -> 11, of which waited for: 9 -> 9; matrix products, arithmetic and copies ran while one was open for 24% -> 29% of each run, Pallas kernels for 0% -> 0%
where the time goes in v1:
time: 2120 us; the launch traced here: 2100 us
  waiting for transfers between devices  1360 us (64%)
  local copies, waits for them, and re-layouts  413 us (19%)
  matrix products  185 us (9%)
  other arithmetic  63.6 us (3%)
  blocking collectives  59.6 us (3%)
    reduce_scatter x1, waiting for transfers between devices, shards(): lax.psum_scatter(row_block(pairs, gains).astype(jnp.bfloat16), 'shard', s...  742 us
    slice x90, local copies, waits for them, and re-layouts, linear_scan(): return lax.associative_scan(combine_steps, (decay, update), axis=0)[1]  194 us
    concatenate x1, local copies, waits for them, and re-layouts, row_block(): return jnp.concatenate(pieces, axis=1)  158 us
    all_gather x1, waiting for transfers between devices, shards(): lax.all_gather(rows_term, 'rep')  123 us
    all_gather x1, waiting for transfers between devices, shards(): lax.all_gather(ffn_gate_weight, 'shard', axis=0, tiled=True)  110 us
    all_gather x1, waiting for transfers between devices, shards(): lax.all_gather(ffn_up_weight, 'shard', axis=0, tiled=True)  106 us
    all_gather x1, waiting for transfers between devices, shards(): lax.all_gather(ffn_down_weight, 'shard', axis=0, tiled=True)  105 us
    all_gather x1, waiting for transfers between devices, shards(): lax.all_gather(forget_weight, 'shard', axis=0, tiled=True)  69 us
  transfers between devices with their start and end apart: 11, of which 9 were waited for; matrix products, arithmetic and copies ran while one was open for 29% of the time, Pallas kernels for 0%

profile of v1, /device:TPU:0, one launch (start us, length us, event | category | flops | bytes accessed | tf_op | source)
XLA Modules:
  0.0 2096.5 jit_solution(15251940753960580753)
XLA Ops:
  12.0 23.2 %all-gather.1 = bf16[16,1,128]{2,1,0:T(2,128)(2,1)S(1)} all-gather(bf16[1,1,128]{2,1,0:T(2,128)(2,1)S(1)} %bitcast.77), channel_id=1, replica_groups=mesh['rep'=2,'shard'=16] {'shard'}, dimensions={0}, use_global_device_ids=true | all-gather | bytes 4352 | tf_op jit(solution)/shard_map/all_gather | solution.py:116
  35.2 17.5 all-gather.2
  52.7 18.9 all-gather.3
  72.6 15.3 all-gather.13.cloned.1.call-done
  87.9 6.4 fusion.57
  94.3 69.0 %all-gather.15.cloned.1.call-done = bf16[2048,2048]{1,0:T(8,128)(2,1)} async-done(((bf16[128,2048]{1,0:T(8,128)(2,1)}), bf16[2048,2048]{1,0:T(8,128)(2,1)}) %all-gather.15.cloned.1.call-update) | async-done | bytes 8388624 | tf_op jit(solution)/shard_map/all_gather | solution.py:114
  163.3 7.8 broadcast_multiply_fusion
  171.0 2.4 slice.393
  177.8 4.6 slice.444
  194.2 2.2 fusion.64
  253.8 2.3 pad.101
  257.5 7.7 multiply_multiply_fusion.1
  265.2 48.6 %all-gather.19.cloned.1.call-done = bf16[2048,2048]{1,0:T(8,128)(2,1)} async-done(((bf16[128,2048]{1,0:T(8,128)(2,1)}), bf16[2048,2048]{1,0:T(8,128)(2,1)}) %all-gather.19.cloned.1.call-update) | async-done | bytes 8388624 | tf_op jit(solution)/shard_map/all_gather | solution.py:132
  313.8 5.9 multiply_reduce_fusion.4
  322.0 110.3 %all-gather.21.cloned.1.call-done = bf16[2048,5632]{1,0:T(8,128)(2,1)} async-done(((bf16[128,5632]{1,0:T(8,128)(2,1)}), bf16[2048,5632]{1,0:T(8,128)(2,1)}) %all-gather.21.cloned.1.call-update) | async-done | bytes 23068688 | tf_op jit(solution)/shard_map/all_gather | solution.py:142
  432.2 14.5 fusion.73
  446.7 105.7 %all-gather.23.cloned.1.call-done = bf16[2048,5632]{1,0:T(8,128)(2,1)} async-done(((bf16[128,5632]{1,0:T(8,128)(2,1)}), bf16[2048,5632]{1,0:T(8,128)(2,1)}) %all-gather.23.cloned.1.call-update) | async-done | bytes 23068688 | tf_op jit(solution)/shard_map/all_gather | solution.py:143
  552.4 15.0 fusion.74
  567.4 105.4 %all-gather.25.cloned.1.call-done = bf16[5632,2048]{1,0:T(8,128)(2,1)} async-done(((bf16[352,2048]{1,0:T(8,128)(2,1)}), bf16[5632,2048]{1,0:T(8,128)(2,1)}) %all-gather.25.cloned.1.call-update) | async-done | bytes 23068688 | tf_op jit(solution)/shard_map/all_gather | solution.py:152
  672.8 16.0 multiply_convert_fusion
  690.1 10.9 convolution_convert_fusion.1
  703.9 4.4 slice.447
  708.3 4.5 slice.456
  712.8 4.5 slice.449
  717.3 8.7 slice.448
  726.0 8.6 slice.457
  734.6 8.6 slice.450
  745.4 12.1 fusion.75
  757.6 14.4 multiply_reduce_fusion
  771.9 2.2 multiply_add_fusion
  775.1 8.6 multiply_reduce_fusion.1
  790.8 8.6 slice.454
  799.4 8.5 slice.452
  807.9 3.2 fusion.61
  811.1 2.7 slice.463
  813.9 2.7 slice.459
  816.5 2.7 slice.461
  819.3 2.7 slice.460
  822.0 2.2 fusion.63
  869.4 2.8 slice.501
  872.3 2.8 slice.458
  877.2 8.7 slice.504
  892.5 2.3 pad.114
  894.8 5.2 pad.115
  900.0 2.9 add.311
  902.9 16.2 rev.6
  919.1 5.8 convolution_convert_fusion.3
  924.9 12.3 copy.30
  937.2 4.1 multiply_convert_fusion.4
  941.3 6.6 fusion.76
  948.0 2.9 convolution_add_fusion.1
  951.0 4.3 fusion.24
  958.7 13.5 convolution_convert_fusion.2
  972.2 20.8 convolution_convert_fusion
  993.0 158.1 %concatenate.84 = bf16[2048,19459]{1,0:T(8,128)(2,1)} concatenate(bf16[2048,6144]{1,0:T(8,128)(2,1)} %convolution_convert_fusion.2, bf16[2048,2048]{1,0:T(8,128)(2,1)} %copy.30, bf16[2048,11264]{1,0:T(8,128)(2,1)} %convolution_convert_fusion, bf16[2048,1]{1,0:T(8,128)(2,1)S(1)} %copy-done.21, bf16[2048,1]{1,0:T(8,128)(2,1)S(1)} %copy-done.22, bf16[2048,1]{1,0:T(8,128)(2,1)} %broadcast_in_dim.20), dimensions={1} | concatenate | bytes 159408128 | tf_op jit(solution)/shard_map/concatenate | solution.py:83
  1151.8 742.3 %reduce-scatter.3.cloned.1.call-done = bf16[128,19459]{1,0:T(8,128)(2,1)} async-done(((bf16[2048,19459]{1,0:T(8,128)(2,1)}), bf16[128,19459]{1,0:T(8,128)(2,1)}) %reduce-scatter.3.cloned.1.call-update) | async-done | bytes 4981520 | tf_op jit(solution)/shard_map/reduce_scatter | solution.py:202
  1894.1 2.9 fusion.28
  1897.0 11.7 fusion.8
  1908.7 35.3 %all-reduce.32.cloned.1.call-done = bf16[352,2048]{1,0:T(8,128)(2,1)} async-done(((bf16[352,2048]{1,0:T(8,128)(2,1)}), bf16[352,2048]{1,0:T(8,128)(2,1)}) %all-reduce.32.cloned.1.call-update) | async-done | bytes 1441808 | tf_op jit(solution)/shard_map/psum | solution.py:210
  1944.0 3.3 convert_element_type.97
  1947.3 122.9 %all-gather.27.cloned.1.call-done = bf16[256,19459]{1,0:T(8,128)(2,1)} async-done(((bf16[128,19459]{1,0:T(8,128)(2,1)}), bf16[256,19459]{1,0:T(8,128)(2,1)}) %all-gather.27.cloned.1.call-update) | async-done | bytes 9963024 | tf_op jit(solution)/shard_map/all_gather | solution.py:209
  2070.1 9.6 reduce_sum.102
  2079.7 3.2 convert_element_type.95
  2085.8 3.2 fusion.59
  (328 shorter events, 158.2 us)
Async XLA Ops:
  7.2 80.7 %all-gather.13.cloned.1.call-start = ((), (), s32[]{:S(2)}) async-start(), calls=%async_computation.2 | async-start | bytes 8912896 | tf_op jit(solution)/shard_map/all_gather | solution.py:113
  7.9 155.3 %all-gather.15.cloned.1.call-start = ((), (), s32[]{:S(2)}) async-start(), calls=%async_computation.3 | async-start | bytes 8912896 | tf_op jit(solution)/shard_map/all_gather | solution.py:114
  8.7 248.8 %all-gather.17.cloned.1.call-start = ((), (), s32[]{:S(2)}) async-start(), calls=%async_computation.4 | async-start | bytes 8912896 | tf_op jit(solution)/shard_map/all_gather | solution.py:115
  9.4 304.4 %all-gather.19.cloned.1.call-start = ((), (), s32[]{:S(2)}) async-start(), calls=%async_computation.5 | async-start | bytes 8912896 | tf_op jit(solution)/shard_map/all_gather | solution.py:132
  10.0 422.3 %all-gather.21.cloned.1.call-start = ((), (), s32[]{:S(2)}) async-start(), calls=%async_computation.6 | async-start | bytes 24510464 | tf_op jit(solution)/shard_map/all_gather | solution.py:142
  10.6 1.4 copy-start.60
  10.6 24.7 %copy-start.61 = (bf16[128]{0:T(256)(128)(2,1)S(1)}, bf16[128]{0:T(256)(128)(2,1)}, u32[]{:S(2)}) copy-start(bf16[128]{0:T(256)(128)(2,1)} %param.19) | copy-start | bytes 772
  10.6 42.1 %copy-start.62 = (bf16[128]{0:T(256)(128)(2,1)S(1)}, bf16[128]{0:T(256)(128)(2,1)}, u32[]{:S(2)}) copy-start(bf16[128]{0:T(256)(128)(2,1)} %param.21) | copy-start | bytes 772
  10.6 61.6 %copy-start.59 = (s32[1,192]{1,0:T(1,128)S(1)}, s32[1,192]{1,0:T(1,128)}, u32[]{:S(2)}) copy-start(s32[1,192]{1,0:T(1,128)} %param.14) | copy-start | bytes 2308
  10.6 61.8 %copy-start.1 = (bf16[1,192,2048]{2,1,0:T(8,128)(2,1)S(1)}, bf16[1,192,2048]{2,1,0:T(8,128)(2,1)}, u32[]{:S(2)}) copy-start(bf16[1,192,2048]{2,1,0:T(8,128)(2,1)} %param.13) | copy-start | bytes 2359300
  10.6 541.8 %all-gather.23.cloned.1.call-start = ((), (), s32[]{:S(2)}) async-start(), calls=%async_computation.7 | async-start | bytes 24510464 | tf_op jit(solution)/shard_map/all_gather | solution.py:143
  11.2 661.6 %all-gather.25.cloned.1.call-start = ((), (), s32[]{:S(2)}) async-start(), calls=%async_computation.8 | async-start | bytes 24510464 | tf_op jit(solution)/shard_map/all_gather | solution.py:152
  11.9 1139.3 %reduce-scatter.5.cloned.1.call-start = ((), (), s32[]{:S(2)}) async-start(), calls=%async_computation.10 | async-start | bytes 24510464 | tf_op jit(solution)/shard_map/reduce_scatter | solution.py:205
  72.4 90.9 %copy-start.57 = (f32[192]{0:T(256)}, f32[192]{0:T(256)S(1)}, u32[]{:S(2)}) copy-start(f32[192]{0:T(256)S(1)} %add_convert_fusion) | copy-start | bytes 2308
  72.6 90.6 %copy-start.42 = (f32[192]{0:T(256)}, f32[192]{0:T(256)S(1)}, u32[]{:S(2)}) copy-start(f32[192]{0:T(256)S(1)} %add_rsqrt_fusion.2) | copy-start | bytes 2308
  171.0 4.6 copy-start.3
  177.8 4.6 copy-start.10
  243.6 5.6 copy-start.31
  243.6 5.6 copy-start.32
  244.8 4.5 copy-start.52
  251.2 1.7 copy-start.15
  256.1 1.4 copy-start.43
  313.8 7.1 copy-start.39
  319.7 1.1 copy-start.5
  672.8 17.3 copy-start.17
  688.7 1.3 copy-start.8
  701.0 1193.0 %reduce-scatter.3.cloned.1.call-start = ((), (), s32[]{:S(2)}) async-start(), calls=%async_computation.9 | async-start | bytes 85229568 | tf_op jit(solution)/shard_map/reduce_scatter | solution.py:202
  743.2 2.2 copy-start.20
  745.4 12.2 copy-start.6
  771.9 2.2 copy-start.4
  771.9 2.7 copy-start.18
  771.9 3.2 copy-start.23
  869.4 16.5 copy-start.35
  869.4 16.5 copy-start.36
  869.4 16.5 copy-start.37
  869.4 16.5 copy-start.38
  872.2 13.9 copy-start.40
  872.2 13.9 copy-start.41
  872.2 14.0 copy-start.54
  872.2 14.1 copy-start.33
  872.2 14.1 copy-start.34
  875.1 11.3 copy-start.53
  887.8 1.2 copy-start.47
  889.2 1.4 copy-start.13
  889.2 1.7 copy-start.16
  902.9 16.2 copy-start.19
  924.9 12.3 copy-start.58
  937.2 10.8 slice-start
  941.3 6.6 copy-start.12
  941.3 6.6 slice-start.1
  941.3 9.6 slice-start.2
  948.0 2.9 copy-start.2
  948.0 2.9 slice-start.3
  948.0 2.9 copy-start.11
  948.0 2.9 copy-start.44
  951.0 5.4 copy-start.56
  951.0 6.6 copy-start.55
  972.1 20.9 copy-start.21
  972.1 20.9 copy-start.22
  1151.1 792.9 %all-reduce.32.cloned.1.call-start = ((), (), s32[]{:S(2)}) async-start(), calls=%async_computation.11 | async-start | bytes 2883584 | tf_op jit(solution)/shard_map/psum | solution.py:210
  1151.7 918.4 %all-gather.27.cloned.1.call-start = ((), (), s32[]{:S(2)}) async-start(), calls=%async_computation.12 | async-start | bytes 15040512 | tf_op jit(solution)/shard_map/all_gather | solution.py:209
  1894.1 2.9 copy-start.7
  1894.1 2.9 copy-start.9
  2079.7 3.9 copy-start
  (14 other events, 13.2 us)
Sparse Core Ops, SparseCore 0:
  10.2 77.6 all-gather.12
  90.1 73.1 all-gather.14
  165.4 73.1 all-gather.16
  240.6 73.1 all-gather.18
  315.2 116.9 all-gather.20
  433.7 118.6 all-gather.22
  554.0 118.6 all-gather.24
  701.1 226.8 reduce-scatter.4
  1151.2 742.7 reduce-scatter.2
  1896.2 47.7 all-reduce.31
  1945.6 124.4 all-gather.26
